TPU v7x, 256 devices: a whole 4x4x8 slice. The times are simulated.
256 devices in a mesh: lon: 32 (over x, y, core), bal: 8 (over z).
Axes of the slice: x: 4, y: 4, z: 8, core: 2. Of those that a mesh axis runs over, the one named last changes fastest.
Arguments:
- conc: float32 [524288, 128], P(('lon', 'bal')), may hold values from -6 to 6
- neighbours: int32 [4096, 8], P(('lon', 'bal')), may hold values from 0 to 4095, as said below
- counts: int32 [4096], P(('lon', 'bal')), may hold values from 1 to 8
- weights: int32 [4096, 8], P(('lon', 'bal')), may hold values from 1 to 15
- zones: int32 [524288], P(('lon', 'bal')), may hold values from 0 to 31
- owners: int32 [524288, 1], P(('lon', 'bal')), may hold values from 0 to 7; in each aligned block of 2048 rows (0 to 2047, 2048 to 4095, ...) at most 512 rows name the same one
- rate_table: float32 [32, 128], replicated, may hold values from 0.05 to 1
- reaction: bfloat16 [128, 128], replicated, may hold values from -0.5 to 0.5
Outputs:
- conc_out: bfloat16 [524288, 128], P(('lon', 'bal'))
- chem_slots: bfloat16 [1048576, 128], P(('lon', 'bal'))
Inputs may be any that keep to these rules, and one draw needn't show every extreme that they name: neighbours[g, k] is a block of the same bal index as g, on the same longitude band or on the band just before or after it, with the bands wrapping around. On every trajectory owner, at most 512 of its parcels have the same owners value; on some trajectory owners one value is taken exactly 512 times.
All inputs are finite; a program needn't handle non-finite values.
Results may differ from a plain program's by a relative error of at most 0.0085.
Values may be sent and summed in bfloat16 or wider, within the bound.
A program may use at most 64 MiB of HBM per device.

v0:
```python
import jax
import jax.numpy as jnp
from jax import lax
from jax.sharding import PartitionSpec as P

BLK = 128
KADJ = 8
ZONES = 32
SUBSTEPS = 12


def extended_2(cells, sides, width):
    for axis, dim in sides:
        count = lax.axis_size(axis)
        head = lax.slice_in_dim(cells, 0, width, axis=dim)
        tail = lax.slice_in_dim(cells, cells.shape[dim] - width, cells.shape[dim], axis=dim)
        cells = jnp.concatenate(
            [
                lax.ppermute(tail, axis, [(i, (i + 1) % count) for i in range(count)]),
                cells,
                lax.ppermute(head, axis, [((i + 1) % count, i) for i in range(count)]),
            ],
            axis=dim,
        )
    return cells


def shifted(value, axis, steps):
    count = lax.axis_size(axis)
    pairs = [(source, (source + steps) % count) for source in range(count)]
    return lax.ppermute(value, axis, pairs)


def chemistry(state, reaction):

    def advance(step_index, current):
        tendency = jnp.dot(
            current.astype(jnp.bfloat16), reaction, preferred_element_type=jnp.float32
        )
        return current + 0.25 * jnp.tanh(tendency)

    return lax.fori_loop(0, SUBSTEPS, advance, state.astype(jnp.float32)).astype(jnp.bfloat16)


def shards(conc, neighbours, counts, weights, zones, owners, rate_table, reaction):
    rows, width = conc.shape
    nblocks = rows // BLK
    lon_count = lax.axis_size("lon")
    bal_count = lax.axis_size("bal")
    device_count = lon_count * bal_count
    self_device = lax.axis_index("lon") * bal_count + lax.axis_index("bal")
    own_blocks = conc.reshape(nblocks, BLK, width)
    extended = extended_2(own_blocks, (("lon", 0),), nblocks)
    used = jnp.arange(KADJ, dtype=jnp.int32)[None, :] < counts[:, None]
    coefs = jnp.where(used, weights.astype(jnp.float32) / 128.0, 0.0)
    local_part = neighbours % nblocks
    apart = (neighbours // nblocks - self_device + device_count) % device_count
    ext_index = (
        jnp.where(apart == 0, nblocks, jnp.where(apart == bal_count, 2 * nblocks, 0)) + local_part
    )
    change = jnp.zeros((nblocks, BLK, width), jnp.float32)
    sent = jnp.zeros((3 * nblocks, BLK, width), jnp.float32)
    for column in range(KADJ):
        flux = coefs[:, column][:, None, None] * (extended[ext_index[:, column]] - own_blocks)
        change = change + flux
        sent = sent.at[ext_index[:, column]].add(flux)
    from_right = shifted(sent[:nblocks].astype(jnp.bfloat16), "lon", -1).astype(jnp.float32)
    from_left = shifted(sent[2 * nblocks :].astype(jnp.bfloat16), "lon", 1).astype(jnp.float32)
    change = change - sent[nblocks : 2 * nblocks] - from_right - from_left
    mixed = (own_blocks + change).reshape(rows, width)
    zone_table = (zones[:, None] == jnp.arange(ZONES, dtype=jnp.int32)[None, :]).astype(jnp.float32)
    rates = jnp.dot(zone_table, rate_table, precision=lax.Precision.HIGHEST)
    moved = (mixed * jnp.exp(-rates)).astype(jnp.bfloat16)
    capacity = 2 * rows // bal_count
    owner = owners[:, 0]
    owner_table = (owner[:, None] == jnp.arange(bal_count, dtype=jnp.int32)[None, :]).astype(
        jnp.int32
    )
    rank = jnp.sum((jnp.cumsum(owner_table, axis=0) - owner_table) * owner_table, axis=1)
    slot = owner * capacity + rank
    conc_out = chemistry(moved, reaction)
    outgoing = jnp.zeros((bal_count * capacity, width), jnp.bfloat16).at[slot].set(conc_out)
    outgoing = outgoing.reshape(bal_count, capacity, width)
    chem_slots = lax.all_to_all(outgoing, "bal", split_axis=0, concat_axis=0, tiled=True).reshape(
        -1, width
    )
    return (conc_out, chem_slots)


def solution(mesh):
    in_specs = (
        P(("lon", "bal"), None),
        P(("lon", "bal"), None),
        P(("lon", "bal")),
        P(("lon", "bal"), None),
        P(("lon", "bal")),
        P(("lon", "bal"), None),
        P(),
        P(),
    )
    out_specs = (P(("lon", "bal"), None), P(("lon", "bal"), None))
    return jax.shard_map(shards, mesh=mesh, in_specs=in_specs, out_specs=out_specs, check_vma=False)
```

profile of v0, /device:TPU:29, one launch (start us, length us, event | category | flops | bytes accessed | tf_op | source)
XLA Modules:
  0.0 125.7 jit_solution(8865160713723251285)
XLA Ops:
  3.3 2.3 %reduce-window.6 = s32[8,16,128]{2,1,0:T(8,128)S(1)} reduce-window(s32[8,16,128]{2,1,0:T(8,128)S(1)} %fusion.15, s32[]{:T(128)} %copy.28), window={size=1x1x128 pad=0_0x0_0x127_0}, to_apply=%region_10.11 | reduce-window | flops 2080768 | bytes 131076 | tf_op jit(solution)/shard_map/reduce-window
  6.8 7.1 %collective-permute-done = f32[16,128,128]{2,1,0:T(8,128)S(1)} collective-permute-done((f32[16,128,128]{2,1,0:T(8,128)}, f32[16,128,128]{2,1,0:T(8,128)S(1)}, u32[]{:S(2)}, u32[]{:S(2)}) %collective-permute-start) | collective-permute-done | bytes 1048608 | tf_op jit(solution)/shard_map/ppermute | solution.py:19
  14.9 3.6 %collective-permute-done.1 = f32[16,128,128]{2,1,0:T(8,128)} collective-permute-done((f32[16,128,128]{2,1,0:T(8,128)}, f32[16,128,128]{2,1,0:T(8,128)}, u32[]{:S(2)}, u32[]{:S(2)}) %collective-permute-start.1) | collective-permute-done | bytes 1048608 | tf_op jit(solution)/shard_map/ppermute | solution.py:21
  18.5 2.1 %pad_maximum_fusion = f32[48,128,128]{2,1,0:T(8,128)S(1)} fusion(f32[16,128,128]{2,1,0:T(8,128)} %collective-permute-done.1, f32[16,128,128]{2,1,0:T(8,128)} %bitcast.70, f32[16,128,128]{2,1,0:T(8,128)} %copy-done.7), kind=kLoop, calls=%fused_computation.21 | loop fusion | flops 1572864 | bytes 6291456 | tf_op jit(solution)/shard_map/concatenate | solution.py:17
  20.6 1.6 %gather_fusion = f32[16,128,128]{2,1,0:T(8,128)} fusion(f32[48,128,128]{2,1,0:T(8,128)S(1)} %pad_maximum_fusion, s32[1024]{0:T(1024)S(1)} %get-tuple-element.59), kind=kCustom, calls=%fused_computation | custom fusion | bytes 2097216 | tf_op jit(solution)/shard_map/gather | solution.py:64
  22.2 1.6 %gather_fusion.1 = f32[16,128,128]{2,1,0:T(8,128)} fusion(f32[48,128,128]{2,1,0:T(8,128)S(1)} %pad_maximum_fusion, s32[1024]{0:T(1024)S(1)} %get-tuple-element.58), kind=kCustom, calls=%fused_computation.1 | custom fusion | bytes 2097216 | tf_op jit(solution)/shard_map/gather | solution.py:64
  28.6 1.6 %gather_fusion.5 = f32[16,128,128]{2,1,0:T(8,128)} fusion(f32[48,128,128]{2,1,0:T(8,128)S(1)} %pad_maximum_fusion, s32[1024]{0:T(1024)S(1)} %get-tuple-element.54), kind=kCustom, calls=%fused_computation.5 | custom fusion | bytes 2097216 | tf_op jit(solution)/shard_map/gather | solution.py:64
  30.2 1.6 %gather_fusion.6 = f32[16,128,128]{2,1,0:T(8,128)} fusion(f32[48,128,128]{2,1,0:T(8,128)S(1)} %pad_maximum_fusion, s32[1024]{0:T(1024)S(1)} %get-tuple-element.53), kind=kCustom, calls=%fused_computation.6 | custom fusion | bytes 2097216 | tf_op jit(solution)/shard_map/gather | solution.py:64
  33.4 7.7 %subtract_multiply_fusion = (f32[16,128,128]{2,1,0:T(8,128)}, f32[16,128,128]{2,1,0:T(8,128)}, f32[16,128,128]{2,1,0:T(8,128)}, f32[16,128,128]{2,1,0:T(8,128)},...) fusion(f32[16,128,128]{2,1,0:T(8,128)} %gather_fusion.7, ...), kind=kLoop, calls=%fused_computation.31 | loop fusion | flops 4194304 | bytes 17826304 | tf_op jit(solution)/shard_map/mul | solution.py:64
  41.5 2.6 %scatter_fusion = f32[48,128,128]{2,1,0:T(8,128)S(1)} fusion(f32[48,128,128]{2,1,0:T(8,128)S(1)} %broadcast_in_dim.18, s32[16]{0:T(128)S(1)} %get-tuple-element.51, f32[16,128,128]{2,1,0:T(8,128)} %get-tuple-element.35), kind=kCustom, calls=%fused_computation.8 | custom fusion | flops 262144 | bytes 3145792 | tf_op jit(solution)/shard_map/scatter-add | solution.py:66
  44.2 2.6 %scatter_fusion.1 = f32[48,128,128]{2,1,0:T(8,128)S(1)} fusion(f32[48,128,128]{2,1,0:T(8,128)S(1)} %scatter_fusion, s32[16]{0:T(128)S(1)} %get-tuple-element.50, f32[16,128,128]{2,1,0:T(8,128)} %get-tuple-element.34), kind=kCustom, calls=%fused_computation.9 | custom fusion | flops 262144 | bytes 3145792 | tf_op jit(solution)/shard_map/scatter-add | solution.py:66
  46.8 2.6 %scatter_fusion.2 = f32[48,128,128]{2,1,0:T(8,128)S(1)} fusion(f32[48,128,128]{2,1,0:T(8,128)S(1)} %scatter_fusion.1, s32[16]{0:T(128)S(1)} %get-tuple-element.49, f32[16,128,128]{2,1,0:T(8,128)} %get-tuple-element.33), kind=kCustom, calls=%fused_computation.10 | custom fusion | flops 262144 | bytes 3145792 | tf_op jit(solution)/shard_map/scatter-add | solution.py:66
  49.4 2.6 %scatter_fusion.3 = f32[48,128,128]{2,1,0:T(8,128)S(1)} fusion(f32[48,128,128]{2,1,0:T(8,128)S(1)} %scatter_fusion.2, s32[16]{0:T(128)S(1)} %get-tuple-element.48, f32[16,128,128]{2,1,0:T(8,128)} %get-tuple-element.32), kind=kCustom, calls=%fused_computation.11 | custom fusion | flops 262144 | bytes 3145792 | tf_op jit(solution)/shard_map/scatter-add | solution.py:66
  52.0 2.6 %scatter_fusion.4 = f32[48,128,128]{2,1,0:T(8,128)S(1)} fusion(f32[48,128,128]{2,1,0:T(8,128)S(1)} %scatter_fusion.3, s32[16]{0:T(128)S(1)} %get-tuple-element.47, f32[16,128,128]{2,1,0:T(8,128)} %get-tuple-element.31), kind=kCustom, calls=%fused_computation.12 | custom fusion | flops 262144 | bytes 3145792 | tf_op jit(solution)/shard_map/scatter-add | solution.py:66
  54.6 2.6 %scatter_fusion.5 = f32[48,128,128]{2,1,0:T(8,128)S(1)} fusion(f32[48,128,128]{2,1,0:T(8,128)S(1)} %scatter_fusion.4, s32[16]{0:T(128)S(1)} %get-tuple-element.46, f32[16,128,128]{2,1,0:T(8,128)} %get-tuple-element.30), kind=kCustom, calls=%fused_computation.13 | custom fusion | flops 262144 | bytes 3145792 | tf_op jit(solution)/shard_map/scatter-add | solution.py:66
  57.2 2.6 %scatter_fusion.6 = f32[48,128,128]{2,1,0:T(8,128)S(1)} fusion(f32[48,128,128]{2,1,0:T(8,128)S(1)} %scatter_fusion.5, s32[16]{0:T(128)S(1)} %get-tuple-element.45, f32[16,128,128]{2,1,0:T(8,128)} %get-tuple-element.29), kind=kCustom, calls=%fused_computation.14 | custom fusion | flops 262144 | bytes 3145792 | tf_op jit(solution)/shard_map/scatter-add | solution.py:66
  59.9 2.6 %scatter_fusion.7 = f32[48,128,128]{2,1,0:T(8,128)S(1)} fusion(f32[48,128,128]{2,1,0:T(8,128)S(1)} %scatter_fusion.6, s32[16]{0:T(128)S(1)} %get-tuple-element.44, f32[16,128,128]{2,1,0:T(8,128)} %get-tuple-element.28), kind=kCustom, calls=%fused_computation.15 | custom fusion | flops 262144 | bytes 3145792 | tf_op jit(solution)/shard_map/scatter-add | solution.py:66
  63.2 3.8 %collective-permute-start.3 = (bf16[16,128,128]{2,1,0:T(8,128)(2,1)S(1)}, bf16[16,128,128]{2,1,0:T(8,128)(2,1)S(1)}, u32[]{:S(2)}, u32[]{:S(2)}) collective-permute-start(bf16[16,128,128]{2,1,0:T(8,128)(2,1)S(1)} %get-tuple-element.27), channel_id=1, source_target_pairs={{0,8},{8,16},{16,24},{24,32},{32,40},{40,48},{48,56},{56,64},{64,7... | collective-permute-start | bytes 1572872 | tf_op jit(solution)/shard_map/ppermute | solution.py:31
  67.1 6.8 %collective-permute-done.2 = bf16[16,128,128]{2,1,0:T(8,128)(2,1)S(1)} collective-permute-done((bf16[16,128,128]{2,1,0:T(8,128)(2,1)S(1)}, bf16[16,128,128]{2,1,0:T(8,128)(2,1)S(1)}, u32[]{:S(2)}, u32[]{:S(2)}) %collective-permute-start.2) | collective-permute-done | bytes 524320 | tf_op jit(solution)/shard_map/ppermute | solution.py:31
  73.9 3.1 %fusion.6 = f32[16,128,128]{2,1,0:T(8,128)S(1)} fusion(f32[16,128,128]{2,1,0:T(8,128)} %bitcast.72, f32[48,128,128]{2,1,0:T(8,128)S(1)} %scatter_fusion.7, bf16[16,128,128]{2,1,0:T(8,128)(2,1)S(1)} %collective-permute-done.3, bf16[16,128,128]{2,1,0:T(8,128)(2,1)S(1)} %collective-permute-done.2, f32[16,128,128]{2,1,0:T(8,128)S(1)} %copy-done.1, ...), kind=kLoop, calls=%fused_computation.27 | loop fusion | flops 3407872 | bytes 12582912 | tf_op jit(solution)/shard_map/add | solution.py:70
  78.1 4.7 %while.10 = (s32[]{:T(128)}, f32[2048,128]{1,0:T(8,128)S(1)}, bf16[128,128]{1,0:T(8,128)(2,1)S(1)}, s32[]{:T(128)}) while((s32[]{:T(128)}, f32[2048,128]{1,0:T(8,128)S(1)}, bf16[128,128]{1,0:T(8,128)(2,1)S(1)}, s32[]{:T(128)}) %tuple.53), condition=%wide.region_9.10_spmd, body=%wide.region_8.9_spmd.sunk | while | flops 67895296 | bytes 4227125 | solution.py:42
  82.7 6.8 %scatter_custom_fusion.8 = bf16[4096,128]{1,0:T(8,128)(2,1)} fusion(s32[2048]{0:T(1024)S(1)} %bitcast.78, bf16[]{:T(256)} %constant.79.clone.1, f32[2048,128]{1,0:T(8,128)S(1)} %get-tuple-element.19), kind=kCustom, calls=%fused_computation.40 | custom fusion | flops 262144 | bytes 2097154 | tf_op jit(solution)/shard_map/scatter | solution.py:82
  89.5 8.2 %all-to-all-start = ((bf16[8,512,128]{2,1,0:T(8,128)(2,1)}), bf16[8,512,128]{2,1,0:T(8,128)(2,1)S(1)}, u32[]{:S(2)}, u32[]{:S(2)}) async-start(bf16[8,512,128]{2,1,0:T(8,128)(2,1)} %bitcast.23), calls=%async_computation | async-start | bytes 2097152 | tf_op jit(solution)/shard_map/all_to_all | solution.py:84
  98.6 26.1 %all-to-all-done = bf16[8,512,128]{2,1,0:T(8,128)(2,1)S(1)} async-done(((bf16[8,512,128]{2,1,0:T(8,128)(2,1)}), bf16[8,512,128]{2,1,0:T(8,128)(2,1)S(1)}, u32[]{:S(2)}, u32[]{:S(2)}) %all-to-all-start) | async-done | bytes 1048608 | tf_op jit(solution)/shard_map/all_to_all | solution.py:84
  (74 shorter events, 19.5 us)
Async XLA Ops:
  0.6 76.4 %copy-start = (f32[32,128]{1,0:T(8,128)S(1)}, f32[32,128]{1,0:T(8,128)}, u32[]{:S(2)}) copy-start(f32[32,128]{1,0:T(8,128)} %param.16) | copy-start | bytes 49156
  0.6 13.3 %collective-permute-start = (f32[16,128,128]{2,1,0:T(8,128)}, f32[16,128,128]{2,1,0:T(8,128)S(1)}, u32[]{:S(2)}, u32[]{:S(2)}) collective-permute-start(f32[16,128,128]{2,1,0:T(8,128)} %bitcast.68), channel_id=1, source_target_pairs={{0,8},{8,16},{16,24},{24,32},{32,40},{40,48},{48,56},{56,64},{64,7... | collective-permute-start | bytes 3145736 | tf_op jit(solution)/shard_map/ppermute | solution.py:19
  1.9 16.6 %collective-permute-start.1 = (f32[16,128,128]{2,1,0:T(8,128)}, f32[16,128,128]{2,1,0:T(8,128)}, u32[]{:S(2)}, u32[]{:S(2)}) collective-permute-start(f32[16,128,128]{2,1,0:T(8,128)} %bitcast.69), channel_id=1, source_target_pairs={{8,0},{16,8},{24,16},{32,24},{40,32},{48,40},{56,48},{64,56},{72,6... | collective-permute-start | bytes 3145736 | tf_op jit(solution)/shard_map/ppermute | solution.py:21
  13.9 1.0 copy-start.7
  62.5 4.5 %copy-start.9 = (s32[2048,1]{0,1:T(1,128)S(1)}, s32[2048,1]{0,1:T(1,128)}, u32[]{:S(2)}) copy-start(s32[2048,1]{0,1:T(1,128)} %param.15) | copy-start | bytes 24580
  62.5 11.4 %copy-start.1 = (f32[16,128,128]{2,1,0:T(8,128)S(1)}, f32[16,128,128]{2,1,0:T(8,128)}, u32[]{:S(2)}) copy-start(f32[16,128,128]{2,1,0:T(8,128)} %get-tuple-element.28) | copy-start | bytes 3145732
  62.5 11.4 %copy-start.2 = (f32[16,128,128]{2,1,0:T(8,128)S(1)}, f32[16,128,128]{2,1,0:T(8,128)}, u32[]{:S(2)}) copy-start(f32[16,128,128]{2,1,0:T(8,128)} %get-tuple-element.29) | copy-start | bytes 3145732
  62.5 11.4 %copy-start.3 = (f32[16,128,128]{2,1,0:T(8,128)S(1)}, f32[16,128,128]{2,1,0:T(8,128)}, u32[]{:S(2)}) copy-start(f32[16,128,128]{2,1,0:T(8,128)} %get-tuple-element.30) | copy-start | bytes 3145732
  62.5 11.4 %copy-start.4 = (f32[16,128,128]{2,1,0:T(8,128)S(1)}, f32[16,128,128]{2,1,0:T(8,128)}, u32[]{:S(2)}) copy-start(f32[16,128,128]{2,1,0:T(8,128)} %get-tuple-element.31) | copy-start | bytes 3145732
  62.5 11.4 %copy-start.5 = (f32[16,128,128]{2,1,0:T(8,128)S(1)}, f32[16,128,128]{2,1,0:T(8,128)}, u32[]{:S(2)}) copy-start(f32[16,128,128]{2,1,0:T(8,128)} %get-tuple-element.32) | copy-start | bytes 3145732
  62.5 11.4 %copy-start.6 = (f32[16,128,128]{2,1,0:T(8,128)S(1)}, f32[16,128,128]{2,1,0:T(8,128)}, u32[]{:S(2)}) copy-start(f32[16,128,128]{2,1,0:T(8,128)} %get-tuple-element.33) | copy-start | bytes 3145732
  62.9 11.0 %collective-permute-start.2 = (bf16[16,128,128]{2,1,0:T(8,128)(2,1)S(1)}, bf16[16,128,128]{2,1,0:T(8,128)(2,1)S(1)}, u32[]{:S(2)}, u32[]{:S(2)}) collective-permute-start(bf16[16,128,128]{2,1,0:T(8,128)(2,1)S(1)} %get-tuple-element.26), channel_id=1, source_target_pairs={{0,248},{8,0},{16,8},{24,16},{32,24},{40,32},{48,40},{56,48},{64,5... | collective-permute-start | bytes 1572872 | tf_op jit(solution)/shard_map/ppermute | solution.py:31
  63.2 10.7 %collective-permute-start.3 = (bf16[16,128,128]{2,1,0:T(8,128)(2,1)S(1)}, bf16[16,128,128]{2,1,0:T(8,128)(2,1)S(1)}, u32[]{:S(2)}, u32[]{:S(2)}) collective-permute-start(bf16[16,128,128]{2,1,0:T(8,128)(2,1)S(1)} %get-tuple-element.27), channel_id=1, source_target_pairs={{0,8},{8,16},{16,24},{24,32},{32,40},{40,48},{48,56},{56,64},{64,7... | collective-permute-start | bytes 1572872 | tf_op jit(solution)/shard_map/ppermute | solution.py:31
  67.1 9.9 %copy-start.10 = (s32[2048]{0:T(1024)S(1)}, s32[2048]{0:T(1024)}, u32[]{:S(2)}) copy-start(s32[2048]{0:T(1024)} %param.14) | copy-start | bytes 24580
  67.1 11.0 %copy-start.8 = (bf16[128,128]{1,0:T(8,128)(2,1)S(1)}, bf16[128,128]{1,0:T(8,128)(2,1)}, u32[]{:S(2)}) copy-start(bf16[128,128]{1,0:T(8,128)(2,1)} %param.17) | copy-start | bytes 98308
  89.5 35.2 %all-to-all-start = ((bf16[8,512,128]{2,1,0:T(8,128)(2,1)}), bf16[8,512,128]{2,1,0:T(8,128)(2,1)S(1)}, u32[]{:S(2)}, u32[]{:S(2)}) async-start(bf16[8,512,128]{2,1,0:T(8,128)(2,1)} %bitcast.23), calls=%async_computation | async-start | bytes 2097152 | tf_op jit(solution)/shard_map/all_to_all | solution.py:84
where the time goes:
time: 126 us
  other arithmetic  46.3 us (37%)
  waiting for transfers between devices  43.6 us (35%)
  local copies, waits for them, and re-layouts  16.4 us (13%)
  starting transfers between devices  13.5 us (11%)
  matrix products  4.52 us (4%)
    all_to_all x1, waiting for transfers between devices, shards(): lax.all_to_all(outgoing, 'bal', split_axis=0, concat_axis=0, tiled=True)  26.1 us
    scatter-add x8, other arithmetic, shards(): sent = sent.at[ext_index[:, column]].add(flux)  20.9 us
    gather x8, local copies, waits for them, and re-layouts, shards(): extended[ext_index[:, column]] - own_blocks  12.9 us
    all_to_all x1, starting transfers between devices, shards(): lax.all_to_all(outgoing, 'bal', split_axis=0, concat_axis=0, tiled=True)  8.18 us
    mul x1, other arithmetic, shards(): coefs[:, column][:, None, None]  7.75 us
    ppermute x1, waiting for transfers between devices, extended_2(): lax.ppermute(tail, axis, [(i, (i + 1) % count) for i in range(count)])  7.07 us
    scatter x1, other arithmetic, shards(): jnp.zeros((bal_count * capacity, width), jnp.bfloat16).at[slot]  6.78 us
    ppermute x2, waiting for transfers between devices, shifted(): return lax.ppermute(value, axis, pairs)  6.76 us
  transfers between devices with their start and end apart: 5, of which 4 were waited for; matrix products, arithmetic and copies ran while one was open for 5% of the time, Pallas kernels for 0%

commit v1 on v0

v1 whole, which is shorter than its diff:
```python
import functools

import jax
import jax.numpy as jnp
from jax import lax
from jax.experimental import pallas as pl
from jax.experimental.pallas import tpu as pltpu
from jax.sharding import PartitionSpec as P

SUBSTEPS = 12
MESH = pl.DeviceIdType.MESH
F32 = jnp.float32
BF16 = jnp.bfloat16


def dot(a, b):
    return jnp.dot(a, b, preferred_element_type=F32)


def dot_nt(a, b):
    return lax.dot_general(a, b, (((1,), (1,)), ((), ())), preferred_element_type=F32)


def iota(shape, dim):
    return lax.broadcasted_iota(jnp.int32, shape, dim)


def chemistry(start, weights):
    half = start.shape[0] // 2
    width = start.shape[1]
    y = jnp.concatenate([start[:half], start[half:]], axis=1).astype(F32)

    def advance(_, y):
        return y + 0.25 * jnp.tanh(dot(y.astype(BF16), weights))

    y = lax.fori_loop(0, SUBSTEPS, advance, y).astype(BF16)
    return jnp.concatenate([y[:, :width], y[:, width:]], axis=0)


def step_kernel(
    nl, nb, early, conc, near_t, counts, weight_t, zones, owners, rates, reaction, out_conc, out_slots,
    xf, xb, factor, start, result, staged, f_send, f_recv, mix, chem_w,
    load_sem, store_sem, f_sems, halo_sems, slot_sems,
):
    li = lax.axis_index("lon")
    bi = lax.axis_index("bal")
    nblk, blk, width = xf.shape
    kadj = near_t.shape[0]
    nzones = rates.shape[0]
    cap = staged.shape[1]
    rows = nblk * blk
    grp = 16
    left = {"lon": lax.rem(li + nl - 1, nl)}
    right = {"lon": lax.rem(li + 1, nl)}

    def peer(d):
        return {"bal": lax.rem(bi + d, nb)}

    def remote(src, dst, sems, i, device):
        return pltpu.make_async_remote_copy(
            src_ref=src, dst_ref=dst, send_sem=sems.at[0, i], recv_sem=sems.at[1, i],
            device_id=device, device_id_type=MESH,
        )

    load = pltpu.make_async_copy(conc, xf, load_sem)
    load.start()
    barrier = pltpu.get_barrier_semaphore()
    for device in [left, right] + [peer(d) for d in range(1, nb)]:
        pl.semaphore_signal(barrier, inc=1, device_id=device, device_id_type=MESH)

    near = near_t[...]
    band = near // (nblk * nb)
    apart = band - li
    place = jnp.where(
        apart == 0, nblk, jnp.where((apart == 1) | (apart == 1 - nl), 2 * nblk, 0)
    ) + near % nblk
    used = iota((kadj, nblk), 0) < counts[...]
    coef = jnp.where(used, weight_t[...].astype(F32) / 128.0, 0.0)
    which = iota((3 * nblk, nblk), 0)
    ft = jnp.zeros((3 * nblk, nblk), F32)
    for k in range(kadj):
        ft = ft + jnp.where(place[k : k + 1, :] == which, coef[k : k + 1, :], 0.0)
    f_send[...] = jnp.zeros_like(f_send)
    f_send[0, :, :nblk] = ft[:nblk]
    f_send[1, :, :nblk] = ft[2 * nblk :]

    pl.semaphore_wait(barrier, nb + 1)
    to_left = remote(f_send.at[0], f_recv.at[1], f_sems, 0, left)
    to_right = remote(f_send.at[1], f_recv.at[0], f_sems, 1, right)
    to_left.start()
    to_right.start()
    load.wait()
    xb[pl.ds(nblk, nblk)] = xf[...].astype(BF16)
    own_blocks = xb.at[pl.ds(nblk, nblk)]
    halo_left = remote(own_blocks, xb.at[pl.ds(2 * nblk, nblk)], halo_sems, 0, left)
    halo_right = remote(own_blocks, xb.at[pl.ds(0, nblk)], halo_sems, 1, right)
    halo_left.start()
    halo_right.start()

    chem_w[...] = jnp.zeros_like(chem_w)
    chem_w[:width, :width] = reaction[...]
    chem_w[width:, width:] = reaction[...]

    own = owners[...]
    member = jnp.concatenate([(own == o).astype(F32) for o in range(nb)], axis=0)
    member_b = member.astype(BF16)
    before = (iota((blk, blk), 0) < iota((blk, blk), 1)).astype(F32).astype(BF16)
    in_row = dot(member_b, before)
    totals = dot(member_b, jnp.ones((blk, blk), BF16))
    r0, r1 = iota((nb * nblk, nb * nblk), 0), iota((nb * nblk, nb * nblk), 1)
    earlier = ((r0 // nblk == r1 // nblk) & (r1 < r0)).astype(F32).astype(BF16)
    offset = dot(earlier, totals.astype(BF16))
    ranks = (member * (in_row + offset)).reshape(nb, nblk, blk).sum(axis=0)
    slot = own * cap + ranks.astype(jnp.int32)

    table = jnp.exp(-rates[...])
    high = table.astype(BF16)
    rest = table - high.astype(F32)
    mid = rest.astype(BF16)
    low = (rest - mid.astype(F32)).astype(BF16)
    parts = jnp.concatenate([high, mid, low, jnp.zeros_like(low)], axis=0)
    zone_t = zones[...].astype(F32).T.astype(jnp.int32)
    lane = iota((blk, 4 * nzones), 1) % nzones
    for b in range(nblk):
        pick = (zone_t[:, b : b + 1] == lane).astype(F32).astype(BF16)
        factor[b] = dot(pick, parts)

    spread = (iota((nblk * grp, nblk), 0) // grp == iota((nblk * grp, nblk), 1)).astype(F32)
    spread_b = spread.astype(BF16)
    widen = (iota((nblk, nblk * grp), 1) // grp == iota((nblk, nblk * grp), 0)).astype(F32).astype(BF16)
    same = (
        iota((nblk * grp, nblk * grp), 0) % grp == iota((nblk * grp, nblk * grp), 1) % grp
    ).astype(F32)
    ft_b = ft.astype(BF16)
    to_left.wait_recv()
    to_right.wait_recv()
    from_left = f_recv[0, :, :nblk].astype(BF16)
    from_right = f_recv[1, :, :nblk].astype(BF16)
    own_ft = ft_b[nblk : 2 * nblk]
    a_own = (dot(spread_b, own_ft) + dot_nt(spread_b, own_ft)) * (1.0 - spread)
    a_left = dot_nt(spread_b, ft_b[:nblk]) + dot(spread_b, from_left)
    a_right = dot_nt(spread_b, ft_b[2 * nblk :]) + dot(spread_b, from_right)
    keep = 1.0 - jnp.sum(a_own + a_left + a_right, axis=1, keepdims=True)
    for i, a in enumerate((a_left, a_own, a_right)):
        mix[i] = (dot(a.astype(BF16), widen) * same).astype(BF16)

    def group(ref, first, j):
        return ref[pl.ds(first, nblk), pl.ds(pl.multiple_of(j * grp, grp), grp), :].reshape(
            nblk * grp, width
        )

    groups = blk // grp

    def add_own(j, carry):
        at = (pl.ds(0, nblk), pl.ds(pl.multiple_of(j * grp, grp), grp), slice(None))
        mixed = group(xf, 0, j) * keep + dot(mix[1], group(xb, nblk, j))
        xf[at] = mixed.reshape(nblk, grp, width)
        return carry

    lax.fori_loop(0, groups, add_own, 0)
    halo_left.wait_recv()
    halo_right.wait_recv()

    def add_halo(j, carry):
        at = (pl.ds(0, nblk), pl.ds(pl.multiple_of(j * grp, grp), grp), slice(None))
        mixed = (
            group(xf, 0, j)
            + dot(mix[0], group(xb, 0, j))
            + dot(mix[2], group(xb, 2 * nblk, j))
        )
        photo = mixed * group(factor, 0, j)
        start[at] = photo.astype(BF16).reshape(nblk, grp, width)
        return carry

    lax.fori_loop(0, groups, add_halo, 0)

    slot_row = iota((cap, blk), 0)

    def pick_slots(values, d):
        base = lax.rem(bi + d, nb) * cap
        row = slot_row + base
        chosen = jnp.concatenate(
            [(slot[b : b + 1, :] == row).astype(F32).astype(BF16) for b in range(nblk)], axis=1
        )
        return dot(chosen, values).astype(BF16)

    def send(d, i):
        copy = remote(
            staged.at[d], out_slots.at[pl.ds(pl.multiple_of(bi * cap, cap), cap)], slot_sems, i, peer(d)
        )
        copy.start()
        return copy

    order = sorted(range(1, nb), key=lambda d: (-min(d, nb - d), d))
    copies = []
    initial = start[...].reshape(rows, width)
    for d in order[:early]:
        staged[d] = chemistry(pick_slots(initial, d), chem_w[...])
        copies.append(send(d, len(copies)))
    for c in range(4):
        part = rows // 4
        result[pl.ds(c * part, part), :] = chemistry(initial[c * part : (c + 1) * part], chem_w[...])
    final = result[...]
    for d in order[early:]:
        staged[d] = pick_slots(final, d)
        copies.append(send(d, len(copies)))
    save = pltpu.make_async_copy(result, out_conc, store_sem.at[0])
    save.start()
    staged[0] = pick_slots(final, 0)
    keep_own = pltpu.make_async_copy(
        staged.at[0], out_slots.at[pl.ds(pl.multiple_of(bi * cap, cap), cap)], store_sem.at[1]
    )
    keep_own.start()
    for copy in (to_left, to_right, halo_left, halo_right):
        copy.wait_send()
    for copy in copies:
        copy.wait()
    save.wait()
    keep_own.wait()


def solution(mesh):
    nl, nb = mesh.shape["lon"], mesh.shape["bal"]
    early = min(2, nb - 1)

    def shards(conc, neighbours, counts, weights, zones, owners, rate_table, reaction):
        rows, width = conc.shape
        nblk = neighbours.shape[0]
        blk = rows // nblk
        cap = 2 * rows // nb
        vmem = pl.BlockSpec(memory_space=pltpu.VMEM)
        hbm = pl.BlockSpec(memory_space=pltpu.HBM)
        return pl.pallas_call(
            functools.partial(step_kernel, nl, nb, early),
            out_shape=(
                jax.ShapeDtypeStruct((rows, width), BF16),
                jax.ShapeDtypeStruct((nb * cap, width), BF16),
            ),
            in_specs=[hbm] + [vmem] * 7,
            out_specs=(hbm, hbm),
            scratch_shapes=[
                pltpu.VMEM((nblk, blk, width), F32),
                pltpu.VMEM((3 * nblk, blk, width), BF16),
                pltpu.VMEM((nblk, blk, width), F32),
                pltpu.VMEM((nblk, blk, width), BF16),
                pltpu.VMEM((rows, width), BF16),
                pltpu.VMEM((nb, cap, width), BF16),
                pltpu.VMEM((2, nblk, 128), F32),
                pltpu.VMEM((2, nblk, 128), F32),
                pltpu.VMEM((3, nblk * 16, nblk * 16), BF16),
                pltpu.VMEM((2 * width, 2 * width), BF16),
                pltpu.SemaphoreType.DMA,
                pltpu.SemaphoreType.DMA((2,)),
                pltpu.SemaphoreType.DMA((2, 2)),
                pltpu.SemaphoreType.DMA((2, 2)),
                pltpu.SemaphoreType.DMA((2, nb - 1)),
            ],
            compiler_params=pltpu.CompilerParams(
                collective_id=0, has_side_effects=True, vmem_limit_bytes=48 << 20
            ),
        )(
            conc.reshape(nblk, blk, width),
            neighbours.T,
            counts.reshape(1, nblk),
            weights.T,
            zones.reshape(nblk, blk),
            owners.reshape(nblk, blk),
            rate_table,
            reaction,
        )

    in_specs = (
        P(("lon", "bal"), None),
        P(("lon", "bal"), None),
        P(("lon", "bal")),
        P(("lon", "bal"), None),
        P(("lon", "bal")),
        P(("lon", "bal"), None),
        P(),
        P(),
    )
    out_specs = (P(("lon", "bal"), None), P(("lon", "bal"), None))
    return jax.shard_map(shards, mesh=mesh, in_specs=in_specs, out_specs=out_specs, check_vma=False)
```

time: 126 us -> 63.3 us (0.50)
  the two profiles are of different devices: /device:TPU:29 before, /device:TPU:1 now
where the time goes in v1:
time: 63.3 us; the launch traced here: 62.9 us
  Pallas kernels  55.1 us (87%)
  local copies, waits for them, and re-layouts  7.22 us (11%)
  between operations  0.66 us (1%)
    pallas_call x1, Pallas kernels, shards(): pl.pallas_call(functools.partial(step_kernel, nl, nb, early), out_shape=(...  55.1 us
    unnamed x18, local copies, waits for them, and re-layouts  7.22 us

profile of v1, /device:TPU:1, one launch (start us, length us, event | category | flops | bytes accessed | tf_op | source)
XLA Modules:
  0.0 62.9 jit_solution(17680456481765902452)
XLA Ops:
  0.6 0.0 copy-start.3
  0.6 0.0 copy-start.7
  0.7 0.7 %copy-done.3 = s32[2048]{0:T(1024)S(1)} copy-done((s32[2048]{0:T(1024)S(1)}, s32[2048]{0:T(1024)}, u32[]{:S(2)}) %copy-start.3) | copy-done | bytes 8216
  1.3 0.0 copy-done.7
  1.3 0.0 copy-start
  1.3 1.2 %copy-done = f32[2048,128]{1,0:T(8,128)S(1)} copy-done((f32[2048,128]{1,0:T(8,128)S(1)}, f32[2048,128]{1,0:T(8,128)}, u32[]{:S(2)}) %copy-start) | copy-done | bytes 1048600
  2.6 0.0 copy-start.1
  2.6 0.8 %copy-done.1 = bf16[128,128]{1,0:T(8,128)(2,1)S(1)} copy-done((bf16[128,128]{1,0:T(8,128)(2,1)S(1)}, bf16[128,128]{1,0:T(8,128)(2,1)}, u32[]{:S(2)}) %copy-start.1) | copy-done | bytes 32792
  3.3 0.0 copy-start.2
  3.3 0.7 %copy-done.2 = f32[32,128]{1,0:T(8,128)S(1)} copy-done((f32[32,128]{1,0:T(8,128)S(1)}, f32[32,128]{1,0:T(8,128)}, u32[]{:S(2)}) %copy-start.2) | copy-done | bytes 16408
  4.0 0.0 copy-start.4
  4.0 0.7 %copy-done.4 = s32[2048,1]{0,1:T(1,128)S(1)} copy-done((s32[2048,1]{0,1:T(1,128)S(1)}, s32[2048,1]{0,1:T(1,128)}, u32[]{:S(2)}) %copy-start.4) | copy-done | bytes 8216
  4.7 0.0 copy-start.5
  4.7 0.7 %copy-done.5 = s32[16,8]{0,1:T(8,128)S(1)} copy-done((s32[16,8]{0,1:T(8,128)S(1)}, s32[16,8]{0,1:T(8,128)}, u32[]{:S(2)}) %copy-start.5) | copy-done | bytes 536
  5.4 0.0 copy-start.6
  5.4 0.7 %copy-done.6 = s32[16,8]{0,1:T(8,128)S(1)} copy-done((s32[16,8]{0,1:T(8,128)S(1)}, s32[16,8]{0,1:T(8,128)}, u32[]{:S(2)}) %copy-start.6) | copy-done | bytes 536
  6.1 55.1 %shard_map.95 = (bf16[2048,128]{1,0:T(8,128)(2,1)S(1)}, bf16[4096,128]{1,0:T(8,128)(2,1)S(1)}) custom-call(f32[16,128,128]{2,1,0:T(8,128)S(1)} %bitcast.6, s32[8,16]{1,0:T(8,128)S(1)} %bitcast.9, s32[1,16]{1,0:T(1,128)S(1)} %bitcast.11, s32[8,16]{1,0:T(8,128)S(1)} %bitcast.10, s32[16,128]{1,0:T(8,128)S(1)} %bitcast.7, s32[16,128]{1,0:T(8,128)S(1)} %bitcast.8, ...), custom_call_target="tpu_custom_call" | custom-call | tf_op jit(solution)/shard_map/pallas_call | solution.py:233
  61.2 0.8 %copy.12 = bf16[2048,128]{1,0:T(8,128)(2,1)} copy(bf16[2048,128]{1,0:T(8,128)(2,1)S(1)} %get-tuple-element.4) | data formatting | bytes 1048576
  62.0 1.0 %copy.13 = bf16[4096,128]{1,0:T(8,128)(2,1)} copy(bf16[4096,128]{1,0:T(8,128)(2,1)S(1)} %get-tuple-element.5) | data formatting | bytes 2097152
Async XLA Ops:
  0.6 0.7 %copy-start.3 = (s32[2048]{0:T(1024)S(1)}, s32[2048]{0:T(1024)}, u32[]{:S(2)}) copy-start(s32[2048]{0:T(1024)} %param.12) | copy-start | bytes 24580
  0.6 0.7 %copy-start.7 = (s32[16]{0:T(128)S(1)}, s32[16]{0:T(128)}, u32[]{:S(2)}) copy-start(s32[16]{0:T(128)} %param.10) | copy-start | bytes 196
  1.3 1.2 %copy-start = (f32[2048,128]{1,0:T(8,128)S(1)}, f32[2048,128]{1,0:T(8,128)}, u32[]{:S(2)}) copy-start(f32[2048,128]{1,0:T(8,128)} %param.8) | copy-start | bytes 3145732
  2.6 0.8 %copy-start.1 = (bf16[128,128]{1,0:T(8,128)(2,1)S(1)}, bf16[128,128]{1,0:T(8,128)(2,1)}, u32[]{:S(2)}) copy-start(bf16[128,128]{1,0:T(8,128)(2,1)} %reaction.1) | copy-start | bytes 98308
  3.3 0.7 %copy-start.2 = (f32[32,128]{1,0:T(8,128)S(1)}, f32[32,128]{1,0:T(8,128)}, u32[]{:S(2)}) copy-start(f32[32,128]{1,0:T(8,128)} %rates.1) | copy-start | bytes 49156
  4.0 0.7 %copy-start.4 = (s32[2048,1]{0,1:T(1,128)S(1)}, s32[2048,1]{0,1:T(1,128)}, u32[]{:S(2)}) copy-start(s32[2048,1]{0,1:T(1,128)} %param.13) | copy-start | bytes 24580
  4.7 0.7 %copy-start.5 = (s32[16,8]{0,1:T(8,128)S(1)}, s32[16,8]{0,1:T(8,128)}, u32[]{:S(2)}) copy-start(s32[16,8]{0,1:T(8,128)} %param.9) | copy-start | bytes 1540
  5.4 0.7 %copy-start.6 = (s32[16,8]{0,1:T(8,128)S(1)}, s32[16,8]{0,1:T(8,128)}, u32[]{:S(2)}) copy-start(s32[16,8]{0,1:T(8,128)} %param.11) | copy-start | bytes 1540

commit v2 on v1

--- a/solution.py
+++ b/solution.py
@@ -25,21 +25,26 @@
     return lax.broadcasted_iota(jnp.int32, shape, dim)
 
 
-def chemistry(start, weights):
-    half = start.shape[0] // 2
-    width = start.shape[1]
-    y = jnp.concatenate([start[:half], start[half:]], axis=1).astype(F32)
-
-    def advance(_, y):
-        return y + 0.25 * jnp.tanh(dot(y.astype(BF16), weights))
-
-    y = lax.fori_loop(0, SUBSTEPS, advance, y).astype(BF16)
-    return jnp.concatenate([y[:, :width], y[:, width:]], axis=0)
+def chemistry(start, weights, chain=256):
+    rows, width = start.shape
+    half = chain // 2
+    ys = [
+        jnp.concatenate([start[c : c + half], start[c + half : c + chain]], axis=1).astype(F32)
+        for c in range(0, rows, chain)
+    ]
+    for _ in range(SUBSTEPS):
+        ys = [y + 0.25 * jnp.tanh(dot(y.astype(BF16), weights)) for y in ys]
+    out = []
+    for y in ys:
+        y = y.astype(BF16)
+        out += [y[:, :width], y[:, width:]]
+    return jnp.concatenate(out, axis=0)
 
 
 def step_kernel(
-    nl, nb, early, conc, near_t, counts, weight_t, zones, owners, rates, reaction, out_conc, out_slots,
-    xf, xb, factor, start, result, staged, f_send, f_recv, mix, chem_w,
+    nl, nb, conc, near_h, counts_h, weight_h, zones_h, owners_h, rates_h, reaction_h, out_conc, out_slots,
+    near_t, counts, weight_t, zones, owners, rates, reaction,
+    xf, xb, factor, start, result, staged, raw, f_send, f_recv, mix, chem_w,
     load_sem, store_sem, f_sems, halo_sems, slot_sems,
 ):
     li = lax.axis_index("lon")
@@ -62,12 +67,27 @@
             device_id=device, device_id_type=MESH,
         )
 
-    load = pltpu.make_async_copy(conc, xf, load_sem)
+    small = [
+        pltpu.make_async_copy(src, dst, load_sem.at[1 + i])
+        for i, (src, dst) in enumerate(
+            (
+                (near_h, near_t), (counts_h, counts), (weight_h, weight_t), (zones_h, zones),
+                (owners_h, owners), (rates_h, rates), (reaction_h, reaction),
+            )
+        )
+    ]
+    for copy in small[:3]:
+        copy.start()
+    load = pltpu.make_async_copy(conc, xf, load_sem.at[0])
     load.start()
+    for copy in small[3:]:
+        copy.start()
     barrier = pltpu.get_barrier_semaphore()
     for device in [left, right] + [peer(d) for d in range(1, nb)]:
         pl.semaphore_signal(barrier, inc=1, device_id=device, device_id_type=MESH)
 
+    for copy in small[:3]:
+        copy.wait()
     near = near_t[...]
     band = near // (nblk * nb)
     apart = band - li
@@ -84,19 +104,21 @@
     f_send[0, :, :nblk] = ft[:nblk]
     f_send[1, :, :nblk] = ft[2 * nblk :]
 
+    load.wait()
+    xb[pl.ds(nblk, nblk)] = xf[...].astype(BF16)
+    own_blocks = xb.at[pl.ds(nblk, nblk)]
     pl.semaphore_wait(barrier, nb + 1)
     to_left = remote(f_send.at[0], f_recv.at[1], f_sems, 0, left)
     to_right = remote(f_send.at[1], f_recv.at[0], f_sems, 1, right)
     to_left.start()
     to_right.start()
-    load.wait()
-    xb[pl.ds(nblk, nblk)] = xf[...].astype(BF16)
-    own_blocks = xb.at[pl.ds(nblk, nblk)]
     halo_left = remote(own_blocks, xb.at[pl.ds(2 * nblk, nblk)], halo_sems, 0, left)
     halo_right = remote(own_blocks, xb.at[pl.ds(0, nblk)], halo_sems, 1, right)
     halo_left.start()
     halo_right.start()
 
+    for copy in small[3:]:
+        copy.wait()
     chem_w[...] = jnp.zeros_like(chem_w)
     chem_w[:width, :width] = reaction[...]
     chem_w[width:, width:] = reaction[...]
@@ -141,38 +163,30 @@
     a_left = dot_nt(spread_b, ft_b[:nblk]) + dot(spread_b, from_left)
     a_right = dot_nt(spread_b, ft_b[2 * nblk :]) + dot(spread_b, from_right)
     keep = 1.0 - jnp.sum(a_own + a_left + a_right, axis=1, keepdims=True)
-    for i, a in enumerate((a_left, a_own, a_right)):
-        mix[i] = (dot(a.astype(BF16), widen) * same).astype(BF16)
-
-    def group(ref, first, j):
-        return ref[pl.ds(first, nblk), pl.ds(pl.multiple_of(j * grp, grp), grp), :].reshape(
-            nblk * grp, width
-        )
-
-    groups = blk // grp
-
-    def add_own(j, carry):
-        at = (pl.ds(0, nblk), pl.ds(pl.multiple_of(j * grp, grp), grp), slice(None))
-        mixed = group(xf, 0, j) * keep + dot(mix[1], group(xb, nblk, j))
-        xf[at] = mixed.reshape(nblk, grp, width)
-        return carry
-
-    lax.fori_loop(0, groups, add_own, 0)
+    mix_own = (dot(a_own.astype(BF16), widen) * same).astype(BF16)
+    for i, a in enumerate((a_left, a_right)):
+        mix[:, i * nblk * grp : (i + 1) * nblk * grp] = (dot(a.astype(BF16), widen) * same).astype(BF16)
+
+    def pair(ref, first, j):
+        parts = [
+            ref[first : first + nblk, g * grp : (g + 1) * grp, :].reshape(nblk * grp, width)
+            for g in (j, j + 1)
+        ]
+        return jnp.concatenate(parts, axis=1)
+
+    def put_pair(ref, j, value):
+        for g in (j, j + 1):
+            part = value[:, (g - j) * width : (g - j + 1) * width]
+            ref[:, g * grp : (g + 1) * grp, :] = part.reshape(nblk, grp, width)
+
+    for j in range(0, blk // grp, 2):
+        put_pair(xf, j, pair(xf, 0, j) * keep + dot(mix_own, pair(xb, nblk, j)))
     halo_left.wait_recv()
     halo_right.wait_recv()
-
-    def add_halo(j, carry):
-        at = (pl.ds(0, nblk), pl.ds(pl.multiple_of(j * grp, grp), grp), slice(None))
-        mixed = (
-            group(xf, 0, j)
-            + dot(mix[0], group(xb, 0, j))
-            + dot(mix[2], group(xb, 2 * nblk, j))
-        )
-        photo = mixed * group(factor, 0, j)
-        start[at] = photo.astype(BF16).reshape(nblk, grp, width)
-        return carry
-
-    lax.fori_loop(0, groups, add_halo, 0)
+    for j in range(0, blk // grp, 2):
+        halo = jnp.concatenate([pair(xb, 0, j), pair(xb, 2 * nblk, j)], axis=0)
+        photo = (pair(xf, 0, j) + dot(mix[...], halo)) * pair(factor, 0, j)
+        put_pair(start, j, photo.astype(BF16))
 
     slot_row = iota((cap, blk), 0)
 
@@ -184,73 +198,78 @@
         )
         return dot(chosen, values).astype(BF16)
 
-    def send(d, i):
-        copy = remote(
-            staged.at[d], out_slots.at[pl.ds(pl.multiple_of(bi * cap, cap), cap)], slot_sems, i, peer(d)
-        )
+    def place_of(d):
+        return pl.ds(pl.multiple_of(lax.rem(bi + d, nb) * cap, cap), cap)
+
+    copies = []
+
+    def send(src, dst, d):
+        copy = remote(src, dst, slot_sems, len(copies), peer(d))
         copy.start()
-        return copy
-
-    order = sorted(range(1, nb), key=lambda d: (-min(d, nb - d), d))
-    copies = []
+        copies.append(copy)
+
+    far = nb // 2
     initial = start[...].reshape(rows, width)
-    for d in order[:early]:
-        staged[d] = chemistry(pick_slots(initial, d), chem_w[...])
-        copies.append(send(d, len(copies)))
-    for c in range(4):
-        part = rows // 4
-        result[pl.ds(c * part, part), :] = chemistry(initial[c * part : (c + 1) * part], chem_w[...])
-    final = result[...]
-    for d in order[early:]:
-        staged[d] = pick_slots(final, d)
-        copies.append(send(d, len(copies)))
+    staged[far] = pick_slots(initial, far)
+    send(staged.at[far], raw, far)
+    result[...] = chemistry(initial, chem_w[...])
     save = pltpu.make_async_copy(result, out_conc, store_sem.at[0])
     save.start()
+    final = result[...]
+    for d in sorted(set(range(1, nb)) - {far}, key=lambda d: (-min(d, nb - d), d)):
+        staged[d] = pick_slots(final, d)
+        send(staged.at[d], out_slots.at[place_of(0)], d)
     staged[0] = pick_slots(final, 0)
-    keep_own = pltpu.make_async_copy(
-        staged.at[0], out_slots.at[pl.ds(pl.multiple_of(bi * cap, cap), cap)], store_sem.at[1]
-    )
-    keep_own.start()
+    stores = [save, pltpu.make_async_copy(staged.at[0], out_slots.at[place_of(0)], store_sem.at[1])]
+    stores[-1].start()
+    copies[0].wait()
+    staged[far] = chemistry(raw[...], chem_w[...])
+    stores.append(pltpu.make_async_copy(staged.at[far], out_slots.at[place_of(nb - far)], store_sem.at[2]))
+    stores[-1].start()
     for copy in (to_left, to_right, halo_left, halo_right):
         copy.wait_send()
-    for copy in copies:
+    for copy in copies[1:] + stores:
         copy.wait()
-    save.wait()
-    keep_own.wait()
 
 
 def solution(mesh):
     nl, nb = mesh.shape["lon"], mesh.shape["bal"]
-    early = min(2, nb - 1)
 
     def shards(conc, neighbours, counts, weights, zones, owners, rate_table, reaction):
         rows, width = conc.shape
         nblk = neighbours.shape[0]
         blk = rows // nblk
         cap = 2 * rows // nb
-        vmem = pl.BlockSpec(memory_space=pltpu.VMEM)
         hbm = pl.BlockSpec(memory_space=pltpu.HBM)
         return pl.pallas_call(
-            functools.partial(step_kernel, nl, nb, early),
+            functools.partial(step_kernel, nl, nb),
             out_shape=(
                 jax.ShapeDtypeStruct((rows, width), BF16),
                 jax.ShapeDtypeStruct((nb * cap, width), BF16),
             ),
-            in_specs=[hbm] + [vmem] * 7,
+            in_specs=[hbm] * 8,
             out_specs=(hbm, hbm),
             scratch_shapes=[
+                pltpu.VMEM((neighbours.shape[1], nblk), jnp.int32),
+                pltpu.VMEM((1, nblk), jnp.int32),
+                pltpu.VMEM((neighbours.shape[1], nblk), jnp.int32),
+                pltpu.VMEM((nblk, blk), jnp.int32),
+                pltpu.VMEM((nblk, blk), jnp.int32),
+                pltpu.VMEM(rate_table.shape, F32),
+                pltpu.VMEM(reaction.shape, BF16),
                 pltpu.VMEM((nblk, blk, width), F32),
                 pltpu.VMEM((3 * nblk, blk, width), BF16),
                 pltpu.VMEM((nblk, blk, width), F32),
                 pltpu.VMEM((nblk, blk, width), BF16),
                 pltpu.VMEM((rows, width), BF16),
                 pltpu.VMEM((nb, cap, width), BF16),
+                pltpu.VMEM((cap, width), BF16),
                 pltpu.VMEM((2, nblk, 128), F32),
                 pltpu.VMEM((2, nblk, 128), F32),
-                pltpu.VMEM((3, nblk * 16, nblk * 16), BF16),
+                pltpu.VMEM((nblk * 16, 2 * nblk * 16), BF16),
                 pltpu.VMEM((2 * width, 2 * width), BF16),
-                pltpu.SemaphoreType.DMA,
-                pltpu.SemaphoreType.DMA((2,)),
+                pltpu.SemaphoreType.DMA((8,)),
+                pltpu.SemaphoreType.DMA((3,)),
                 pltpu.SemaphoreType.DMA((2, 2)),
                 pltpu.SemaphoreType.DMA((2, 2)),
                 pltpu.SemaphoreType.DMA((2, nb - 1)),

time: 63.3 us -> 52.2 us (0.82)
  Pallas kernels: 55.1 us -> 44 us
    pallas_call x1, Pallas kernels: 55.1 us -> 44 us  [shards(): pl.pallas_call(functools.partial(step_kernel, nl, nb), out_shape=(jax.Sha...]
where the time goes in v2:
time: 52.2 us; the launch traced here: 51.9 us
  Pallas kernels  44 us (84%)
  local copies, waits for them, and re-layouts  7.22 us (14%)
  between operations  0.66 us (1%)
    pallas_call x1, Pallas kernels, shards(): pl.pallas_call(functools.partial(step_kernel, nl, nb), out_shape=(jax.Sha...  44 us
    unnamed x18, local copies, waits for them, and re-layouts  7.22 us

profile of v2, /device:TPU:1, one launch (start us, length us, event | category | flops | bytes accessed | tf_op | source)
XLA Modules:
  0.0 51.9 jit_solution(5574868452413162736)
XLA Ops:
  0.6 0.0 copy-start.3
  0.6 0.0 copy-start.7
  0.7 0.7 %copy-done.3 = s32[2048]{0:T(1024)S(1)} copy-done((s32[2048]{0:T(1024)S(1)}, s32[2048]{0:T(1024)}, u32[]{:S(2)}) %copy-start.3) | copy-done | bytes 8216
  1.3 0.0 copy-done.7
  1.3 0.0 copy-start
  1.3 1.2 %copy-done = f32[2048,128]{1,0:T(8,128)S(1)} copy-done((f32[2048,128]{1,0:T(8,128)S(1)}, f32[2048,128]{1,0:T(8,128)}, u32[]{:S(2)}) %copy-start) | copy-done | bytes 1048600
  2.6 0.0 copy-start.1
  2.6 0.8 %copy-done.1 = bf16[128,128]{1,0:T(8,128)(2,1)S(1)} copy-done((bf16[128,128]{1,0:T(8,128)(2,1)S(1)}, bf16[128,128]{1,0:T(8,128)(2,1)}, u32[]{:S(2)}) %copy-start.1) | copy-done | bytes 32792
  3.3 0.0 copy-start.2
  3.3 0.7 %copy-done.2 = f32[32,128]{1,0:T(8,128)S(1)} copy-done((f32[32,128]{1,0:T(8,128)S(1)}, f32[32,128]{1,0:T(8,128)}, u32[]{:S(2)}) %copy-start.2) | copy-done | bytes 16408
  4.0 0.0 copy-start.4
  4.0 0.7 %copy-done.4 = s32[2048,1]{0,1:T(1,128)S(1)} copy-done((s32[2048,1]{0,1:T(1,128)S(1)}, s32[2048,1]{0,1:T(1,128)}, u32[]{:S(2)}) %copy-start.4) | copy-done | bytes 8216
  4.7 0.0 copy-start.5
  4.7 0.7 %copy-done.5 = s32[16,8]{0,1:T(8,128)S(1)} copy-done((s32[16,8]{0,1:T(8,128)S(1)}, s32[16,8]{0,1:T(8,128)}, u32[]{:S(2)}) %copy-start.5) | copy-done | bytes 536
  5.4 0.0 copy-start.6
  5.4 0.7 %copy-done.6 = s32[16,8]{0,1:T(8,128)S(1)} copy-done((s32[16,8]{0,1:T(8,128)S(1)}, s32[16,8]{0,1:T(8,128)}, u32[]{:S(2)}) %copy-start.6) | copy-done | bytes 536
  6.1 44.0 %shard_map.95 = (bf16[2048,128]{1,0:T(8,128)(2,1)S(1)}, bf16[4096,128]{1,0:T(8,128)(2,1)S(1)}) custom-call(f32[16,128,128]{2,1,0:T(8,128)S(1)} %bitcast.6, s32[8,16]{1,0:T(8,128)S(1)} %bitcast.9, s32[1,16]{1,0:T(1,128)S(1)} %bitcast.11, s32[8,16]{1,0:T(8,128)S(1)} %bitcast.10, s32[16,128]{1,0:T(8,128)S(1)} %bitcast.7, s32[16,128]{1,0:T(8,128)S(1)} %bitcast.8, ...), custom_call_target="tpu_custom_call" | custom-call | tf_op jit(solution)/shard_map/pallas_call | solution.py:244
  50.1 0.8 %copy.12 = bf16[2048,128]{1,0:T(8,128)(2,1)} copy(bf16[2048,128]{1,0:T(8,128)(2,1)S(1)} %get-tuple-element.4) | data formatting | bytes 1048576
  50.9 1.0 %copy.13 = bf16[4096,128]{1,0:T(8,128)(2,1)} copy(bf16[4096,128]{1,0:T(8,128)(2,1)S(1)} %get-tuple-element.5) | data formatting | bytes 2097152
Async XLA Ops:
  0.6 0.7 %copy-start.3 = (s32[2048]{0:T(1024)S(1)}, s32[2048]{0:T(1024)}, u32[]{:S(2)}) copy-start(s32[2048]{0:T(1024)} %param.12) | copy-start | bytes 24580
  0.6 0.7 %copy-start.7 = (s32[16]{0:T(128)S(1)}, s32[16]{0:T(128)}, u32[]{:S(2)}) copy-start(s32[16]{0:T(128)} %param.10) | copy-start | bytes 196
  1.3 1.2 %copy-start = (f32[2048,128]{1,0:T(8,128)S(1)}, f32[2048,128]{1,0:T(8,128)}, u32[]{:S(2)}) copy-start(f32[2048,128]{1,0:T(8,128)} %param.8) | copy-start | bytes 3145732
  2.6 0.8 %copy-start.1 = (bf16[128,128]{1,0:T(8,128)(2,1)S(1)}, bf16[128,128]{1,0:T(8,128)(2,1)}, u32[]{:S(2)}) copy-start(bf16[128,128]{1,0:T(8,128)(2,1)} %reaction_h.1) | copy-start | bytes 98308
  3.3 0.7 %copy-start.2 = (f32[32,128]{1,0:T(8,128)S(1)}, f32[32,128]{1,0:T(8,128)}, u32[]{:S(2)}) copy-start(f32[32,128]{1,0:T(8,128)} %rates_h.1) | copy-start | bytes 49156
  4.0 0.7 %copy-start.4 = (s32[2048,1]{0,1:T(1,128)S(1)}, s32[2048,1]{0,1:T(1,128)}, u32[]{:S(2)}) copy-start(s32[2048,1]{0,1:T(1,128)} %param.13) | copy-start | bytes 24580
  4.7 0.7 %copy-start.5 = (s32[16,8]{0,1:T(8,128)S(1)}, s32[16,8]{0,1:T(8,128)}, u32[]{:S(2)}) copy-start(s32[16,8]{0,1:T(8,128)} %param.9) | copy-start | bytes 1540
  5.4 0.7 %copy-start.6 = (s32[16,8]{0,1:T(8,128)S(1)}, s32[16,8]{0,1:T(8,128)}, u32[]{:S(2)}) copy-start(s32[16,8]{0,1:T(8,128)} %param.11) | copy-start | bytes 1540

commit v3 on v2

--- a/solution.py
+++ b/solution.py
@@ -232,6 +232,18 @@
         copy.wait()
 
 
+def save_kernel(pieces, conc_ref, slots_ref, out_conc, out_slots, sems):
+    copies = []
+    for src, dst in ((slots_ref, out_slots), (conc_ref, out_conc)):
+        part = src.shape[0] // pieces
+        for p in range(pieces):
+            at = pl.ds(p * part, part)
+            copies.append(pltpu.make_async_copy(src.at[at], dst.at[at], sems.at[len(copies)]))
+            copies[-1].start()
+    for copy in copies:
+        copy.wait()
+
+
 def solution(mesh):
     nl, nb = mesh.shape["lon"], mesh.shape["bal"]
 
@@ -241,14 +253,16 @@
         blk = rows // nblk
         cap = 2 * rows // nb
         hbm = pl.BlockSpec(memory_space=pltpu.HBM)
-        return pl.pallas_call(
+        out_shape = (
+            jax.ShapeDtypeStruct((rows, width), BF16),
+            jax.ShapeDtypeStruct((nb * cap, width), BF16),
+        )
+        params = dict(has_side_effects=True, vmem_limit_bytes=48 << 20)
+        done = pl.pallas_call(
             functools.partial(step_kernel, nl, nb),
-            out_shape=(
-                jax.ShapeDtypeStruct((rows, width), BF16),
-                jax.ShapeDtypeStruct((nb * cap, width), BF16),
-            ),
+            out_shape=out_shape,
             in_specs=[hbm] * 8,
-            out_specs=(hbm, hbm),
+            out_specs=(pl.BlockSpec(memory_space=pl.ANY),) * 2,
             scratch_shapes=[
                 pltpu.VMEM((neighbours.shape[1], nblk), jnp.int32),
                 pltpu.VMEM((1, nblk), jnp.int32),
@@ -274,19 +288,31 @@
                 pltpu.SemaphoreType.DMA((2, 2)),
                 pltpu.SemaphoreType.DMA((2, nb - 1)),
             ],
-            compiler_params=pltpu.CompilerParams(
-                collective_id=0, has_side_effects=True, vmem_limit_bytes=48 << 20
-            ),
+            compiler_params=pltpu.CompilerParams(collective_id=0, **params),
         )(
-            conc.reshape(nblk, blk, width),
-            neighbours.T,
-            counts.reshape(1, nblk),
-            weights.T,
-            zones.reshape(nblk, blk),
-            owners.reshape(nblk, blk),
-            rate_table,
-            reaction,
-        )
+            *(
+                pltpu.with_memory_space_constraint(a, pltpu.HBM)
+                for a in (
+                    conc.reshape(nblk, blk, width),
+                    neighbours.T,
+                    counts.reshape(1, nblk),
+                    weights.T,
+                    zones.reshape(nblk, blk),
+                    owners.reshape(nblk, blk),
+                    rate_table,
+                    reaction,
+                )
+            )
+        )
+        pieces = 4
+        return pl.pallas_call(
+            functools.partial(save_kernel, pieces),
+            out_shape=out_shape,
+            in_specs=[pl.BlockSpec(memory_space=pl.ANY)] * 2,
+            out_specs=(hbm, hbm),
+            scratch_shapes=[pltpu.SemaphoreType.DMA((2 * pieces,))],
+            compiler_params=pltpu.CompilerParams(**params),
+        )(*done)
 
     in_specs = (
         P(("lon", "bal"), None),

time: 52.2 us -> 45.9 us (0.88)
  local copies, waits for them, and re-layouts: 7.22 us -> 0 us
  Pallas kernels: 44 us -> 45.2 us
    unnamed x18 -> x0, local copies, waits for them, and re-layouts: 7.22 us -> none
    pallas_call x1 -> x2, Pallas kernels: 44 us -> 45.2 us  [the longest x1 44 us: shards(): pl.pallas_call(functools.partial(step_kernel, nl, nb), out_shape=out_shap...]
where the time goes in v3:
time: 45.9 us; the launch traced here: 45.8 us
  Pallas kernels  45.2 us (98%)
  between operations  0.64 us (1%)
    pallas_call x1, Pallas kernels, shards(): pl.pallas_call(functools.partial(step_kernel, nl, nb), out_shape=out_shap...  44 us
    pallas_call x1, Pallas kernels, shards(): pl.pallas_call(functools.partial(save_kernel, pieces), out_shape=out_shap...  1.2 us

profile of v3, /device:TPU:1, one launch (start us, length us, event | category | flops | bytes accessed | tf_op | source)
XLA Modules:
  0.0 45.8 jit_solution(8880511998528823936)
XLA Ops:
  0.6 44.0 %shard_map.95 = (bf16[2048,128]{1,0:T(8,128)(2,1)S(1)}, bf16[4096,128]{1,0:T(8,128)(2,1)S(1)}) custom-call(f32[16,128,128]{2,1,0:T(8,128)} %bitcast.6, s32[8,16]{1,0:T(8,128)} %bitcast.9, s32[1,16]{1,0:T(1,128)} %bitcast.11, s32[8,16]{1,0:T(8,128)} %bitcast.10, s32[16,128]{1,0:T(8,128)} %bitcast.7, s32[16,128]{1,0:T(8,128)} %bitcast.8, f32[32,128]{1,0:T(8,128)} %rates_h.1, ...), custom_call_target="tpu_custom_call" | custom-call | tf_op jit(solution)/shard_map/pallas_call | solution.py:261
  44.6 1.2 %shard_map.96 = (bf16[2048,128]{1,0:T(8,128)(2,1)}, bf16[4096,128]{1,0:T(8,128)(2,1)}) custom-call(bf16[2048,128]{1,0:T(8,128)(2,1)S(1)} %get-tuple-element.4.conc_ref, bf16[4096,128]{1,0:T(8,128)(2,1)S(1)} %get-tuple-element.5.slots_ref), custom_call_target="tpu_custom_call" | custom-call | tf_op jit(solution)/shard_map/pallas_call | solution.py:308

commit v4 on v3

--- a/solution.py
+++ b/solution.py
@@ -45,7 +45,7 @@
     nl, nb, conc, near_h, counts_h, weight_h, zones_h, owners_h, rates_h, reaction_h, out_conc, out_slots,
     near_t, counts, weight_t, zones, owners, rates, reaction,
     xf, xb, factor, start, result, staged, raw, f_send, f_recv, mix, chem_w,
-    load_sem, store_sem, f_sems, halo_sems, slot_sems,
+    load_sem, store_sem, f_sems, halo_sems, slot_sems, ready,
 ):
     li = lax.axis_index("lon")
     bi = lax.axis_index("bal")
@@ -58,9 +58,6 @@
     left = {"lon": lax.rem(li + nl - 1, nl)}
     right = {"lon": lax.rem(li + 1, nl)}
 
-    def peer(d):
-        return {"bal": lax.rem(bi + d, nb)}
-
     def remote(src, dst, sems, i, device):
         return pltpu.make_async_remote_copy(
             src_ref=src, dst_ref=dst, send_sem=sems.at[0, i], recv_sem=sems.at[1, i],
@@ -83,8 +80,14 @@
     for copy in small[3:]:
         copy.start()
     barrier = pltpu.get_barrier_semaphore()
-    for device in [left, right] + [peer(d) for d in range(1, nb)]:
+    for device in (left, right):
         pl.semaphore_signal(barrier, inc=1, device_id=device, device_id_type=MESH)
+    for d in range(1, nb):
+
+        @pl.when(bi + d < nb)
+        def _():
+            pl.semaphore_signal(barrier, inc=1, device_id={"bal": bi + d}, device_id_type=MESH)
+
 
     for copy in small[:3]:
         copy.wait()
@@ -107,7 +110,7 @@
     load.wait()
     xb[pl.ds(nblk, nblk)] = xf[...].astype(BF16)
     own_blocks = xb.at[pl.ds(nblk, nblk)]
-    pl.semaphore_wait(barrier, nb + 1)
+    pl.semaphore_wait(barrier, 2 + bi)
     to_left = remote(f_send.at[0], f_recv.at[1], f_sems, 0, left)
     to_right = remote(f_send.at[1], f_recv.at[0], f_sems, 1, right)
     to_left.start()
@@ -116,6 +119,11 @@
     halo_right = remote(own_blocks, xb.at[pl.ds(0, nblk)], halo_sems, 1, right)
     halo_left.start()
     halo_right.start()
+    for d in range(1, nb):
+
+        @pl.when(bi - d >= 0)
+        def _():
+            pl.semaphore_signal(ready, inc=1, device_id={"bal": bi - d}, device_id_type=MESH)
 
     for copy in small[3:]:
         copy.wait()
@@ -190,41 +198,49 @@
 
     slot_row = iota((cap, blk), 0)
 
-    def pick_slots(values, d):
-        base = lax.rem(bi + d, nb) * cap
-        row = slot_row + base
+    def pick_slots(values, owner):
+        row = slot_row + owner * cap
         chosen = jnp.concatenate(
             [(slot[b : b + 1, :] == row).astype(F32).astype(BF16) for b in range(nblk)], axis=1
         )
         return dot(chosen, values).astype(BF16)
 
-    def place_of(d):
-        return pl.ds(pl.multiple_of(lax.rem(bi + d, nb) * cap, cap), cap)
+    def slots_from(source):
+        return out_slots.at[pl.ds(pl.multiple_of(source * cap, cap), cap)]
 
     copies = []
 
-    def send(src, dst, d):
-        copy = remote(src, dst, slot_sems, len(copies), peer(d))
+    def send(src, dst, owner):
+        copy = remote(src, dst, slot_sems, len(copies), {"bal": owner})
         copy.start()
         copies.append(copy)
 
-    far = nb // 2
+    half = nb // 2
+    side, place_in = bi // half, lax.rem(bi, half)
+    across = [(1 - side) * half + lax.rem(place_in + k, half) for k in range(half)]
+    within = [side * half + lax.rem(place_in + k, half) for k in range(1, half)]
+
     initial = start[...].reshape(rows, width)
-    staged[far] = pick_slots(initial, far)
-    send(staged.at[far], raw, far)
+    staged[1] = pick_slots(initial, across[0])
+
+    @pl.when(bi < nb - 1)
+    def _():
+        pl.semaphore_wait(ready, nb - 1 - bi)
+
+    send(staged.at[1], raw, across[0])
     result[...] = chemistry(initial, chem_w[...])
     save = pltpu.make_async_copy(result, out_conc, store_sem.at[0])
     save.start()
     final = result[...]
-    for d in sorted(set(range(1, nb)) - {far}, key=lambda d: (-min(d, nb - d), d)):
-        staged[d] = pick_slots(final, d)
-        send(staged.at[d], out_slots.at[place_of(0)], d)
-    staged[0] = pick_slots(final, 0)
-    stores = [save, pltpu.make_async_copy(staged.at[0], out_slots.at[place_of(0)], store_sem.at[1])]
+    for k, owner in enumerate(across[1:] + within):
+        staged[2 + k] = pick_slots(final, owner)
+        send(staged.at[2 + k], slots_from(bi), owner)
+    staged[0] = pick_slots(final, bi)
+    stores = [save, pltpu.make_async_copy(staged.at[0], slots_from(bi), store_sem.at[1])]
     stores[-1].start()
     copies[0].wait()
-    staged[far] = chemistry(raw[...], chem_w[...])
-    stores.append(pltpu.make_async_copy(staged.at[far], out_slots.at[place_of(nb - far)], store_sem.at[2]))
+    staged[1] = chemistry(raw[...], chem_w[...])
+    stores.append(pltpu.make_async_copy(staged.at[1], slots_from(across[0]), store_sem.at[2]))
     stores[-1].start()
     for copy in (to_left, to_right, halo_left, halo_right):
         copy.wait_send()
@@ -287,6 +303,7 @@
                 pltpu.SemaphoreType.DMA((2, 2)),
                 pltpu.SemaphoreType.DMA((2, 2)),
                 pltpu.SemaphoreType.DMA((2, nb - 1)),
+                pltpu.SemaphoreType.REGULAR,
             ],
             compiler_params=pltpu.CompilerParams(collective_id=0, **params),
         )(

time: 45.9 us -> 43.7 us (0.952)
  the two profiles are of different devices: /device:TPU:1 before, /device:TPU:65 now
where the time goes in v4:
time: 43.7 us; the launch traced here: 43.6 us
  Pallas kernels  43 us (98%)
  between operations  0.64 us (1%)
    pallas_call x1, Pallas kernels, shards(): pl.pallas_call(functools.partial(step_kernel, nl, nb), out_shape=out_shap...  41.8 us
    pallas_call x1, Pallas kernels, shards(): pl.pallas_call(functools.partial(save_kernel, pieces), out_shape=out_shap...  1.2 us

profile of v4, /device:TPU:65, one launch (start us, length us, event | category | flops | bytes accessed | tf_op | source)
XLA Modules:
  0.0 43.6 jit_solution(6878995345934889406)
XLA Ops:
  0.6 41.8 %shard_map.95 = (bf16[2048,128]{1,0:T(8,128)(2,1)S(1)}, bf16[4096,128]{1,0:T(8,128)(2,1)S(1)}) custom-call(f32[16,128,128]{2,1,0:T(8,128)} %bitcast.6, s32[8,16]{1,0:T(8,128)} %bitcast.9, s32[1,16]{1,0:T(1,128)} %bitcast.11, s32[8,16]{1,0:T(8,128)} %bitcast.10, s32[16,128]{1,0:T(8,128)} %bitcast.7, s32[16,128]{1,0:T(8,128)} %bitcast.8, f32[32,128]{1,0:T(8,128)} %rates_h.1, ...), custom_call_target="tpu_custom_call" | custom-call | tf_op jit(solution)/shard_map/pallas_call | solution.py:277
  42.4 1.2 %shard_map.96 = (bf16[2048,128]{1,0:T(8,128)(2,1)}, bf16[4096,128]{1,0:T(8,128)(2,1)}) custom-call(bf16[2048,128]{1,0:T(8,128)(2,1)S(1)} %get-tuple-element.4.conc_ref, bf16[4096,128]{1,0:T(8,128)(2,1)S(1)} %get-tuple-element.5.slots_ref), custom_call_target="tpu_custom_call" | custom-call | tf_op jit(solution)/shard_map/pallas_call | solution.py:325

commit v5 on v4

--- a/solution.py
+++ b/solution.py
@@ -41,10 +41,20 @@
     return jnp.concatenate(out, axis=0)
 
 
+def cross(first, second):
+    half = first.shape[-1] // 2
+    low = iota(first.shape, first.ndim - 1) < half
+
+    def turn(v):
+        return pltpu.roll(v, half, v.ndim - 1)
+
+    return jnp.where(low, first, turn(second)), jnp.where(low, turn(first), second)
+
+
 def step_kernel(
     nl, nb, conc, near_h, counts_h, weight_h, zones_h, owners_h, rates_h, reaction_h, out_conc, out_slots,
     near_t, counts, weight_t, zones, owners, rates, reaction,
-    xf, xb, factor, start, result, staged, raw, f_send, f_recv, mix, chem_w,
+    xf, xp, xb, factor, start, result, staged, ahead, raw, f_send, f_recv, mix, chem_w,
     load_sem, store_sem, f_sems, halo_sems, slot_sems, ready,
 ):
     li = lax.axis_index("lon")
@@ -55,6 +65,7 @@
     cap = staged.shape[1]
     rows = nblk * blk
     grp = 16
+    hb = blk // 2
     left = {"lon": lax.rem(li + nl - 1, nl)}
     right = {"lon": lax.rem(li + 1, nl)}
 
@@ -108,17 +119,25 @@
     f_send[1, :, :nblk] = ft[2 * nblk :]
 
     load.wait()
-    xb[pl.ds(nblk, nblk)] = xf[...].astype(BF16)
-    own_blocks = xb.at[pl.ds(nblk, nblk)]
+    for h, packed in enumerate(cross(xf[:, :hb, :], xf[:, hb:, :])):
+        xp[h] = packed
+        xb[h, nblk : 2 * nblk] = packed.astype(BF16)
     pl.semaphore_wait(barrier, 2 + bi)
     to_left = remote(f_send.at[0], f_recv.at[1], f_sems, 0, left)
     to_right = remote(f_send.at[1], f_recv.at[0], f_sems, 1, right)
     to_left.start()
     to_right.start()
-    halo_left = remote(own_blocks, xb.at[pl.ds(2 * nblk, nblk)], halo_sems, 0, left)
-    halo_right = remote(own_blocks, xb.at[pl.ds(0, nblk)], halo_sems, 1, right)
-    halo_left.start()
-    halo_right.start()
+    halos = []
+    for h in range(2):
+        own_blocks = xb.at[h, pl.ds(nblk, nblk)]
+        pair_of = (
+            remote(own_blocks, xb.at[h, pl.ds(2 * nblk, nblk)], halo_sems, 2 * h, left),
+            remote(own_blocks, xb.at[h, pl.ds(0, nblk)], halo_sems, 2 * h + 1, right),
+        )
+        for copy in pair_of:
+            copy.start()
+        halos.append(pair_of)
+
     for d in range(1, nb):
 
         @pl.when(bi - d >= 0)
@@ -153,7 +172,9 @@
     lane = iota((blk, 4 * nzones), 1) % nzones
     for b in range(nblk):
         pick = (zone_t[:, b : b + 1] == lane).astype(F32).astype(BF16)
-        factor[b] = dot(pick, parts)
+        rate = dot(pick, parts)
+        for h, packed in enumerate(cross(rate[:hb], rate[hb:])):
+            factor[h, b] = packed
 
     spread = (iota((nblk * grp, nblk), 0) // grp == iota((nblk * grp, nblk), 1)).astype(F32)
     spread_b = spread.astype(BF16)
@@ -187,23 +208,29 @@
             part = value[:, (g - j) * width : (g - j + 1) * width]
             ref[:, g * grp : (g + 1) * grp, :] = part.reshape(nblk, grp, width)
 
-    for j in range(0, blk // grp, 2):
-        put_pair(xf, j, pair(xf, 0, j) * keep + dot(mix_own, pair(xb, nblk, j)))
-    halo_left.wait_recv()
-    halo_right.wait_recv()
-    for j in range(0, blk // grp, 2):
-        halo = jnp.concatenate([pair(xb, 0, j), pair(xb, 2 * nblk, j)], axis=0)
-        photo = (pair(xf, 0, j) + dot(mix[...], halo)) * pair(factor, 0, j)
-        put_pair(start, j, photo.astype(BF16))
+    for h in range(2):
+        for j in range(0, hb // grp, 2):
+            own_x = xp.at[h]
+            put_pair(own_x, j, pair(own_x, 0, j) * keep + dot(mix_own, pair(xb.at[h], nblk, j)))
 
     slot_row = iota((cap, blk), 0)
 
+    def choose(owner):
+        row = slot_row + owner * cap
+        return jnp.concatenate(
+            [(slot[b : b + 1, :] == row).astype(F32).astype(BF16) for b in range(nblk)], axis=1
+        )
+
     def pick_slots(values, owner):
-        row = slot_row + owner * cap
-        chosen = jnp.concatenate(
-            [(slot[b : b + 1, :] == row).astype(F32).astype(BF16) for b in range(nblk)], axis=1
-        )
-        return dot(chosen, values).astype(BF16)
+        return dot(choose(owner), values).astype(BF16)
+
+    def finish(h):
+        for copy in halos[h]:
+            copy.wait_recv()
+        for j in range(0, hb // grp, 2):
+            halo = jnp.concatenate([pair(xb.at[h], 0, j), pair(xb.at[h], 2 * nblk, j)], axis=0)
+            photo = (pair(xp.at[h], 0, j) + dot(mix[...], halo)) * pair(factor.at[h], 0, j)
+            put_pair(xp.at[h], j, photo.astype(BF16).astype(F32))
 
     def slots_from(source):
         return out_slots.at[pl.ds(pl.multiple_of(source * cap, cap), cap)]
@@ -220,14 +247,23 @@
     across = [(1 - side) * half + lax.rem(place_in + k, half) for k in range(half)]
     within = [side * half + lax.rem(place_in + k, half) for k in range(1, half)]
 
-    initial = start[...].reshape(rows, width)
-    staged[1] = pick_slots(initial, across[0])
+    chosen = choose(across[0])
+    finish(0)
+    start[:, :hb, :], start[:, hb:, :] = (v.astype(BF16) for v in cross(xp[0], xp[0]))
+    rows_low = dot(chosen, start[...].reshape(rows, width))
+    ahead[0] = cross(rows_low[: cap // 2], rows_low[cap // 2 :])[0].astype(BF16)
 
     @pl.when(bi < nb - 1)
     def _():
         pl.semaphore_wait(ready, nb - 1 - bi)
 
-    send(staged.at[1], raw, across[0])
+    send(ahead.at[0], raw.at[0], across[0])
+    finish(1)
+    start[:, :hb, :], start[:, hb:, :] = (v.astype(BF16) for v in cross(xp[0], xp[1]))
+    initial = start[...].reshape(rows, width)
+    rows_all = dot(chosen, initial)
+    ahead[1] = cross(rows_all[: cap // 2], rows_all[cap // 2 :])[1].astype(BF16)
+    send(ahead.at[1], raw.at[1], across[0])
     result[...] = chemistry(initial, chem_w[...])
     save = pltpu.make_async_copy(result, out_conc, store_sem.at[0])
     save.start()
@@ -238,13 +274,15 @@
     staged[0] = pick_slots(final, bi)
     stores = [save, pltpu.make_async_copy(staged.at[0], slots_from(bi), store_sem.at[1])]
     stores[-1].start()
-    copies[0].wait()
-    staged[1] = chemistry(raw[...], chem_w[...])
+    for copy in copies[:2]:
+        copy.wait()
+    arrived = jnp.concatenate(cross(raw[0].astype(F32), raw[1].astype(F32)), axis=0).astype(BF16)
+    staged[1] = chemistry(arrived, chem_w[...])
     stores.append(pltpu.make_async_copy(staged.at[1], slots_from(across[0]), store_sem.at[2]))
     stores[-1].start()
-    for copy in (to_left, to_right, halo_left, halo_right):
+    for copy in (to_left, to_right) + halos[0] + halos[1]:
         copy.wait_send()
-    for copy in copies[1:] + stores:
+    for copy in copies[2:] + stores:
         copy.wait()
 
 
@@ -288,12 +326,14 @@
                 pltpu.VMEM(rate_table.shape, F32),
                 pltpu.VMEM(reaction.shape, BF16),
                 pltpu.VMEM((nblk, blk, width), F32),
-                pltpu.VMEM((3 * nblk, blk, width), BF16),
-                pltpu.VMEM((nblk, blk, width), F32),
+                pltpu.VMEM((2, nblk, blk // 2, width), F32),
+                pltpu.VMEM((2, 3 * nblk, blk // 2, width), BF16),
+                pltpu.VMEM((2, nblk, blk // 2, width), F32),
                 pltpu.VMEM((nblk, blk, width), BF16),
                 pltpu.VMEM((rows, width), BF16),
                 pltpu.VMEM((nb, cap, width), BF16),
-                pltpu.VMEM((cap, width), BF16),
+                pltpu.VMEM((2, cap // 2, width), BF16),
+                pltpu.VMEM((2, cap // 2, width), BF16),
                 pltpu.VMEM((2, nblk, 128), F32),
                 pltpu.VMEM((2, nblk, 128), F32),
                 pltpu.VMEM((nblk * 16, 2 * nblk * 16), BF16),
@@ -301,8 +341,8 @@
                 pltpu.SemaphoreType.DMA((8,)),
                 pltpu.SemaphoreType.DMA((3,)),
                 pltpu.SemaphoreType.DMA((2, 2)),
-                pltpu.SemaphoreType.DMA((2, 2)),
-                pltpu.SemaphoreType.DMA((2, nb - 1)),
+                pltpu.SemaphoreType.DMA((2, 4)),
+                pltpu.SemaphoreType.DMA((2, nb)),
                 pltpu.SemaphoreType.REGULAR,
             ],
             compiler_params=pltpu.CompilerParams(collective_id=0, **params),

time: 43.7 us -> 42.7 us (0.977)
  Pallas kernels: 43 us -> 42 us
    pallas_call x1, Pallas kernels: 41.8 us -> 40.8 us  [shards(): pl.pallas_call(functools.partial(step_kernel, nl, nb), out_shape=out_shap...]
where the time goes in v5:
time: 42.7 us; the launch traced here: 42.6 us
  Pallas kernels  42 us (98%)
  between operations  0.64 us (1%)
    pallas_call x1, Pallas kernels, shards(): pl.pallas_call(functools.partial(step_kernel, nl, nb), out_shape=out_shap...  40.8 us
    pallas_call x1, Pallas kernels, shards(): pl.pallas_call(functools.partial(save_kernel, pieces), out_shape=out_shap...  1.2 us

profile of v5, /device:TPU:65, one launch (start us, length us, event | category | flops | bytes accessed | tf_op | source)
XLA Modules:
  0.0 42.6 jit_solution(13720867024303627597)
XLA Ops:
  0.6 40.8 %shard_map.95 = (bf16[2048,128]{1,0:T(8,128)(2,1)S(1)}, bf16[4096,128]{1,0:T(8,128)(2,1)S(1)}) custom-call(f32[16,128,128]{2,1,0:T(8,128)} %bitcast.6, s32[8,16]{1,0:T(8,128)} %bitcast.9, s32[1,16]{1,0:T(1,128)} %bitcast.11, s32[8,16]{1,0:T(8,128)} %bitcast.10, s32[16,128]{1,0:T(8,128)} %bitcast.7, s32[16,128]{1,0:T(8,128)} %bitcast.8, f32[32,128]{1,0:T(8,128)} %rates_h.1, ...), custom_call_target="tpu_custom_call" | custom-call | tf_op jit(solution)/shard_map/pallas_call | solution.py:315
  41.4 1.2 %shard_map.96 = (bf16[2048,128]{1,0:T(8,128)(2,1)}, bf16[4096,128]{1,0:T(8,128)(2,1)}) custom-call(bf16[2048,128]{1,0:T(8,128)(2,1)S(1)} %get-tuple-element.4.conc_ref, bf16[4096,128]{1,0:T(8,128)(2,1)S(1)} %get-tuple-element.5.slots_ref), custom_call_target="tpu_custom_call" | custom-call | tf_op jit(solution)/shard_map/pallas_call | solution.py:365

commit v6 on v5

--- a/solution.py
+++ b/solution.py
@@ -247,42 +247,50 @@
     across = [(1 - side) * half + lax.rem(place_in + k, half) for k in range(half)]
     within = [side * half + lax.rem(place_in + k, half) for k in range(1, half)]
 
-    chosen = choose(across[0])
+    early = raw.shape[0]
+    chosen = [choose(across[k]) for k in range(early)]
     finish(0)
     start[:, :hb, :], start[:, hb:, :] = (v.astype(BF16) for v in cross(xp[0], xp[0]))
-    rows_low = dot(chosen, start[...].reshape(rows, width))
-    ahead[0] = cross(rows_low[: cap // 2], rows_low[cap // 2 :])[0].astype(BF16)
-
-    @pl.when(bi < nb - 1)
-    def _():
-        pl.semaphore_wait(ready, nb - 1 - bi)
-
-    send(ahead.at[0], raw.at[0], across[0])
+
+    def send_half(k, h):
+        picked = dot(chosen[k], start[...].reshape(rows, width))
+        ahead[k, h] = cross(picked[: cap // 2], picked[cap // 2 :])[h].astype(BF16)
+        if k + h == 0:
+
+            @pl.when(bi < nb - 1)
+            def _():
+                pl.semaphore_wait(ready, nb - 1 - bi)
+
+        send(ahead.at[k, h], raw.at[k, h], across[k])
+
+    for k in range(early):
+        send_half(k, 0)
     finish(1)
     start[:, :hb, :], start[:, hb:, :] = (v.astype(BF16) for v in cross(xp[0], xp[1]))
+    for k in range(early):
+        send_half(k, 1)
     initial = start[...].reshape(rows, width)
-    rows_all = dot(chosen, initial)
-    ahead[1] = cross(rows_all[: cap // 2], rows_all[cap // 2 :])[1].astype(BF16)
-    send(ahead.at[1], raw.at[1], across[0])
     result[...] = chemistry(initial, chem_w[...])
     save = pltpu.make_async_copy(result, out_conc, store_sem.at[0])
     save.start()
     final = result[...]
-    for k, owner in enumerate(across[1:] + within):
-        staged[2 + k] = pick_slots(final, owner)
-        send(staged.at[2 + k], slots_from(bi), owner)
+    for k, owner in enumerate(across[early:] + within, early):
+        staged[1 + k] = pick_slots(final, owner)
+        send(staged.at[1 + k], slots_from(bi), owner)
     staged[0] = pick_slots(final, bi)
     stores = [save, pltpu.make_async_copy(staged.at[0], slots_from(bi), store_sem.at[1])]
     stores[-1].start()
-    for copy in copies[:2]:
-        copy.wait()
-    arrived = jnp.concatenate(cross(raw[0].astype(F32), raw[1].astype(F32)), axis=0).astype(BF16)
-    staged[1] = chemistry(arrived, chem_w[...])
-    stores.append(pltpu.make_async_copy(staged.at[1], slots_from(across[0]), store_sem.at[2]))
-    stores[-1].start()
+    for k in range(early):
+        for h in range(2):
+            copies[k + h * early].wait()
+        arrived = jnp.concatenate(cross(raw[k, 0].astype(F32), raw[k, 1].astype(F32)), axis=0)
+        staged[1 + k] = chemistry(arrived.astype(BF16), chem_w[...])
+        source = (1 - side) * half + lax.rem(place_in + half - k, half)
+        stores.append(pltpu.make_async_copy(staged.at[1 + k], slots_from(source), store_sem.at[2 + k]))
+        stores[-1].start()
     for copy in (to_left, to_right) + halos[0] + halos[1]:
         copy.wait_send()
-    for copy in copies[2:] + stores:
+    for copy in copies[2 * early :] + stores:
         copy.wait()
 
 
@@ -300,6 +308,7 @@
 
 def solution(mesh):
     nl, nb = mesh.shape["lon"], mesh.shape["bal"]
+    early = min(2, nb // 2)
 
     def shards(conc, neighbours, counts, weights, zones, owners, rate_table, reaction):
         rows, width = conc.shape
@@ -332,17 +341,17 @@
                 pltpu.VMEM((nblk, blk, width), BF16),
                 pltpu.VMEM((rows, width), BF16),
                 pltpu.VMEM((nb, cap, width), BF16),
-                pltpu.VMEM((2, cap // 2, width), BF16),
-                pltpu.VMEM((2, cap // 2, width), BF16),
+                pltpu.VMEM((early, 2, cap // 2, width), BF16),
+                pltpu.VMEM((early, 2, cap // 2, width), BF16),
                 pltpu.VMEM((2, nblk, 128), F32),
                 pltpu.VMEM((2, nblk, 128), F32),
                 pltpu.VMEM((nblk * 16, 2 * nblk * 16), BF16),
                 pltpu.VMEM((2 * width, 2 * width), BF16),
                 pltpu.SemaphoreType.DMA((8,)),
-                pltpu.SemaphoreType.DMA((3,)),
+                pltpu.SemaphoreType.DMA((2 + early,)),
                 pltpu.SemaphoreType.DMA((2, 2)),
                 pltpu.SemaphoreType.DMA((2, 4)),
-                pltpu.SemaphoreType.DMA((2, nb)),
+                pltpu.SemaphoreType.DMA((2, nb - 1 + early)),
                 pltpu.SemaphoreType.REGULAR,
             ],
             compiler_params=pltpu.CompilerParams(collective_id=0, **params),

time: 42.7 us -> 41.4 us (0.970)
  the two profiles are of different devices: /device:TPU:65 before, /device:TPU:64 now
where the time goes in v6:
time: 41.4 us; the launch traced here: 41.2 us
  Pallas kernels  40.6 us (98%)
  between operations  0.64 us (2%)
    pallas_call x1, Pallas kernels, shards(): pl.pallas_call(functools.partial(step_kernel, nl, nb), out_shape=out_shap...  39.4 us
    pallas_call x1, Pallas kernels, shards(): pl.pallas_call(functools.partial(save_kernel, pieces), out_shape=out_shap...  1.2 us

profile of v6, /device:TPU:64, one launch (start us, length us, event | category | flops | bytes accessed | tf_op | source)
XLA Modules:
  0.0 41.2 jit_solution(12790504185483465682)
XLA Ops:
  0.6 39.4 %shard_map.95 = (bf16[2048,128]{1,0:T(8,128)(2,1)S(1)}, bf16[4096,128]{1,0:T(8,128)(2,1)S(1)}) custom-call(f32[16,128,128]{2,1,0:T(8,128)} %bitcast.6, s32[8,16]{1,0:T(8,128)} %bitcast.9, s32[1,16]{1,0:T(1,128)} %bitcast.11, s32[8,16]{1,0:T(8,128)} %bitcast.10, s32[16,128]{1,0:T(8,128)} %bitcast.7, s32[16,128]{1,0:T(8,128)} %bitcast.8, f32[32,128]{1,0:T(8,128)} %rates_h.1, ...), custom_call_target="tpu_custom_call" | custom-call | tf_op jit(solution)/shard_map/pallas_call | solution.py:324
  40.0 1.2 %shard_map.96 = (bf16[2048,128]{1,0:T(8,128)(2,1)}, bf16[4096,128]{1,0:T(8,128)(2,1)}) custom-call(bf16[2048,128]{1,0:T(8,128)(2,1)S(1)} %get-tuple-element.4.conc_ref, bf16[4096,128]{1,0:T(8,128)(2,1)S(1)} %get-tuple-element.5.slots_ref), custom_call_target="tpu_custom_call" | custom-call | tf_op jit(solution)/shard_map/pallas_call | solution.py:374
